TPU v7x, 32 devices: a whole 2x2x4 slice. The times are simulated.
32 devices in a mesh: rep: 1, seq: 16 (over z, y, core), head: 2 (over x).
Axes of the slice: x: 2, y: 2, z: 4, core: 2. Of those that a mesh axis runs over, the one named last changes fastest.
Arguments:
- states: bfloat16 [256, 8192], P('rep', 'seq'), may hold values from -6 to 6
- w_query: bfloat16 [8192, 8192], P('seq', 'head'), may hold values from -0.0625 to 0.0625
- w_key: bfloat16 [8192, 1024], P('seq', 'head'), may hold values from -0.3125 to 0.3125
- w_value: bfloat16 [8192, 1024], P('seq', 'head'), may hold values from -0.25 to 0.25
- w_out: bfloat16 [8192, 8192], P('head', 'seq'), may hold values from -0.09375 to 0.09375
- key_cache: bfloat16 [2, 8192, 1024], P('rep', 'seq', 'head'), may hold values from -480 to 480
- value_cache: bfloat16 [2, 8192, 1024], P('rep', 'seq', 'head'), may hold values from -24 to 24
- parents: int32 [2, 128], P('rep'), may hold values from 0 to 126, as said below
- cache_lengths: int32 [2], P('rep'), may hold values from 2048 to 8192, as said below
Outputs:
- attended: bfloat16 [256, 8192], P('rep', ('seq', 'head'))
Inputs may be any that keep to these rules, and one draw needn't show every extreme that they name: parents[t, 0] = 0, parents[t, i] < i for i >= 1, and the last node's parent is node 126. `cache_lengths`: at least one sequence fills all 8192 positions.
All inputs are finite; a program needn't handle non-finite values.
Results may differ from a plain program's by a relative error of at most 0.014.
The roundings to bfloat16 on the way count: a program that leaves them out, or rounds other values in their place, can miss the bound.
Values may be sent and summed in bfloat16 or wider, within the bound.
No kernel may reach another device: no remote copies, remote signals or barrier semaphores. Data moves between devices by JAX's collectives and lax.ppermute only.
A program may use at most 320 MiB of HBM per device.

v0:
```python
import jax
import jax.numpy as jnp
from jax import lax
from jax.sharding import PartitionSpec as P

HEAD_DIM = 128
rope_base = 500000.0
neg_big = -1e30


def ancestry(parents):
    count = parents.shape[1]
    ident = jnp.eye(count, dtype=jnp.float32)
    onehot = (parents[:, :, None] == jnp.arange(count, dtype=jnp.int32)[None, None, :]).astype(
        jnp.float32
    )
    reach = jnp.minimum(ident[None] + onehot, 1.0)
    for level in range(max(1, (count - 1).bit_length())):
        reach = jnp.minimum(
            jnp.einsum("tij,tjk->tik", reach, reach, precision=lax.Precision.HIGHEST), 1.0
        )
    return reach


def rotate(values, position):
    count = values.shape[0]
    half = HEAD_DIM // 2
    shaped = values.reshape(count, -1, HEAD_DIM)
    freq = rope_base ** (-(jnp.arange(half, dtype=jnp.float32) * 2.0 / HEAD_DIM))
    angle = position[:, None] * freq[None, :]
    cosine = jnp.cos(angle)[:, None, :]
    sine = jnp.sin(angle)[:, None, :]
    first = shaped[..., :half]
    second = shaped[..., half:]
    turned = jnp.concatenate([first * cosine - second * sine, second * cosine + first * sine], -1)
    return turned.reshape(count, -1)


def combine(left, right):
    top = jnp.maximum(left[0], right[0])
    scale_left = jnp.exp(left[0] - top)
    scale_right = jnp.exp(right[0] - top)
    return (
        top,
        left[1] * scale_left + right[1] * scale_right,
        left[2] * scale_left[..., None] + right[2] * scale_right[..., None],
    )


def cache_state(query, keys, values, length, offset):
    total = keys.shape[0]
    block = min(total, 2048)
    count = total // block
    rows_here, kv_local, group, width = query.shape
    scale = width ** (-0.5)
    keys = keys.reshape(count, block, kv_local, width)
    values = values.reshape(count, block, kv_local, width)

    def step(carry, inputs):
        key_block, value_block, first = inputs
        valid = offset + first + jnp.arange(block, dtype=jnp.int32) < length
        scores = (
            jnp.einsum("rkgd,nkd->rkgn", query, key_block, preferred_element_type=jnp.float32)
            * scale
        )
        scores = jnp.where(valid, scores, neg_big)
        top = jnp.maximum(carry[0], jnp.max(scores, -1))
        weights = jnp.where(valid, jnp.exp(scores - top[..., None]), 0.0)
        shrink = jnp.exp(carry[0] - top)
        mass = carry[1] * shrink + jnp.sum(weights, -1)
        acc = carry[2] * shrink[..., None] + jnp.einsum(
            "rkgn,nkd->rkgd",
            weights.astype(jnp.bfloat16),
            value_block,
            preferred_element_type=jnp.float32,
        )
        return ((top, mass, acc), None)

    init = (
        jnp.full((rows_here, kv_local, group), neg_big, jnp.float32),
        jnp.zeros((rows_here, kv_local, group), jnp.float32),
        jnp.zeros((rows_here, kv_local, group, width), jnp.float32),
    )
    firsts = jnp.arange(count, dtype=jnp.int32) * block
    state, _ = lax.scan(step, init, (keys, values, firsts))
    return state


def tree_state(query, new_keys, new_values, allowed):
    rows_here, kv_local, group, width = query.shape
    scale = width ** (-0.5)
    keys = new_keys.reshape(-1, kv_local, width)
    values = new_values.reshape(-1, kv_local, width)
    mask = allowed[:, None, None, :]
    scores = jnp.einsum("rkgd,nkd->rkgn", query, keys, preferred_element_type=jnp.float32) * scale
    scores = jnp.where(mask, scores, neg_big)
    top = jnp.max(scores, -1)
    weights = jnp.where(mask, jnp.exp(scores - top[..., None]), 0.0)
    acc = jnp.einsum(
        "rkgn,nkd->rkgd", weights.astype(jnp.bfloat16), values, preferred_element_type=jnp.float32
    )
    return (top, jnp.sum(weights, -1), acc)


def local(states, w_query, w_key, w_value, w_out, key_cache, value_cache, parents, cache_lengths):
    trees, tree_rows = parents.shape
    rows = trees * tree_rows
    kv_local = key_cache.shape[2] // HEAD_DIM
    heads_local = w_query.shape[1] // HEAD_DIM
    group = heads_local // kv_local
    reach = ancestry(parents)
    position = (cache_lengths.astype(jnp.float32)[:, None] + jnp.sum(reach, -1) - 1.0).reshape(-1)
    allowed = (jnp.eye(trees, dtype=jnp.float32)[:, None, :, None] * reach[:, :, None, :]).reshape(
        rows, rows
    ) > 0.5
    q_part = jnp.dot(states, w_query, preferred_element_type=jnp.float32)
    k_part = jnp.dot(states, w_key, preferred_element_type=jnp.float32)
    v_part = jnp.dot(states, w_value, preferred_element_type=jnp.float32)
    q_raw, k_raw, v_raw = lax.psum((q_part, k_part, v_part), "seq")
    queries = rotate(q_raw, position).astype(jnp.bfloat16)
    new_keys = rotate(k_raw, position).astype(jnp.bfloat16)
    new_values = v_raw.astype(jnp.bfloat16)
    query_heads = queries.reshape(rows, kv_local, group, HEAD_DIM)
    offset = lax.axis_index("seq") * key_cache.shape[1]
    parts_list = []
    for tree in range(trees):
        parts_list.append(
            cache_state(
                query_heads[tree * tree_rows : (tree + 1) * tree_rows],
                key_cache[tree],
                value_cache[tree],
                cache_lengths[tree],
                offset,
            )
        )
    peak = jnp.concatenate([item[0] for item in parts_list], 0)
    mass = jnp.concatenate([item[1] for item in parts_list], 0)
    acc = jnp.concatenate([item[2] for item in parts_list], 0)
    summit = lax.pmax(peak, "seq")
    factor = jnp.exp(peak - summit)
    mass_share, acc_share = (
        lax.psum_scatter(mass * factor, "seq", scatter_dimension=0, tiled=True),
        lax.psum_scatter(acc * factor[..., None], "seq", scatter_dimension=0, tiled=True),
    )
    share = mass_share.shape[0]
    first_row = lax.axis_index("seq") * share
    summit_share = lax.dynamic_slice_in_dim(summit, first_row, share)
    query_share = lax.dynamic_slice_in_dim(query_heads, first_row, share)
    allowed_share = lax.dynamic_slice_in_dim(allowed, first_row, share)
    total = combine(
        (summit_share, mass_share, acc_share),
        tree_state(query_share, new_keys, new_values, allowed_share),
    )
    attention_share = (total[2] / total[1][..., None]).reshape(share, -1).astype(jnp.bfloat16)
    attention = lax.all_gather(attention_share, "seq", axis=0, tiled=True)
    partial_value = jnp.dot(attention, w_out, preferred_element_type=jnp.float32)
    return lax.psum_scatter(partial_value, "head", scatter_dimension=1, tiled=True).astype(
        jnp.bfloat16
    )


def solution(mesh):
    placed = (
        P("rep", "seq"),
        P("seq", "head"),
        P("seq", "head"),
        P("seq", "head"),
        P("head", "seq"),
        P("rep", "seq", "head"),
        P("rep", "seq", "head"),
        P("rep", None),
        P("rep"),
    )
    return jax.shard_map(
        local, mesh=mesh, in_specs=placed, out_specs=P("rep", ("seq", "head")), check_vma=False
    )
```

profile of v0, /device:TPU:0, one launch (start us, length us, event | category | flops | bytes accessed | tf_op | source)
XLA Modules:
  0.0 412.9 jit_solution(16273453118756324011)
XLA Ops:
  6.5 1.0 copy-done
  7.6 1.2 convolution_bitcast_fusion.1
  8.8 0.9 copy.84
  9.7 3.5 convolution_bitcast_fusion
  13.2 2.7 copy.76
  16.0 1.1 copy-done.6
  17.3 0.6 fusion.66
  18.0 1.0 copy.74
  19.2 1.0 copy.72
  20.4 1.8 fusion.47
  22.2 0.4 convolution_minimum_fusion.6
  22.6 0.3 convolution_minimum_fusion.5
  23.7 0.3 convolution_minimum_fusion.1
  24.0 0.4 fusion.67
  24.4 0.5 multiply_cosine_fusion
  25.0 110.8 %all-reduce.4.cloned.1.call-done = (f32[256,4,128]{2,0,1:T(8,128)}, f32[256,32,128]{2,1,0:T(8,128)}) async-done(((f32[256,4,128]{2,0,1:T(8,128)}, f32[256,32,128]{2,1,0:T(8,128)}), (f32[256,4,128]{2,0,1:T(8,128)}, f32[256,32,128]{2,1,0:T(8,128)})) %all-reduce.4.cloned.1.call-update) | async-done | bytes 4718608 | tf_op jit(solution)/shard_map/psum | solution.py:119
  135.7 4.8 %multiply_subtract_fusion = (bf16[256,32,64]{2,1,0:T(8,128)(2,1)S(1)}, bf16[256,32,64]{2,1,0:T(8,128)(2,1)S(1)}) fusion(f32[256,32,128]{2,1,0:T(8,128)} %get-tuple-element.40, f32[256,64]{1,0:T(8,128)S(1)} %get-tuple-element.81, f32[256,64]{1,0:T(8,128)S(1)} %get-tuple-element.80), kind=kLoop, calls=%fused_computation.17 | loop fusion | flops 4194304 | bytes 6422528 | tf_op jit(solution)/shard_map/sub | solution.py:35
  140.6 1.2 maximum_convert_fusion
  141.8 0.4 fusion.63
  142.1 0.4 copy.40
  142.5 1.3 bitcast_reduce_fusion
  143.9 3.1 fusion.6
  147.1 0.6 fusion.60
  147.7 0.4 copy.35
  148.1 1.3 bitcast_reduce_fusion.1
  149.5 2.4 fusion.4
  151.9 0.8 copy-done.3
  152.7 0.6 fusion.59
  153.3 60.0 %pmax.7 = f32[256,4,8]{0,2,1:T(8,128)S(1)} all-reduce(f32[256,4,8]{0,2,1:T(8,128)S(1)} %pad_maximum_fusion), channel_id=1, replica_groups=mesh['rep'=1,'seq'=16,'head'=2] {'seq'}, use_global_device_ids=true, to_apply=%region_4.5 | all-reduce | flops 8192 | bytes 65536 | tf_op jit(solution)/shard_map/pmax | solution.py:139
  213.3 0.6 fusion.43
  213.9 0.8 copy.69
  215.0 5.7 %bitcast_add_fusion = f32[128,4,8,128]{3,0,2,1:T(8,128)S(1)} fusion(bf16[512,4,128,1]{0,2,3,1:T(8,128)(2,1)S(1)} %bitcast.140, f32[4,128,8,512]{3,1,2,0:T(8,128)} %copy-done.2, f32[128,4,8]{0,2,1:T(8,128)S(1)} %broadcast_maximum_fusion, pred[512]{0:T(512)(128)(4,1)} %copy-done.19, f32[128,4,8]{0,2,1:T(8,128)} %get-tuple-element.79), kind=kOutput, calls=%fused_computation.25 | convolution fusion | flops 547880960 | bytes 11043328 | tf_op jit(solution)/shard_map/while/body/eval_jaxpr/rkgn,nkd->rkgd/dot_general | solution.py:71
  220.7 5.5 %bitcast_add_fusion.1 = f32[128,4,8,128]{3,0,2,1:T(8,128)S(1)} fusion(bf16[512,4,128,1]{0,2,3,1:T(8,128)(2,1)S(1)} %bitcast.139, f32[4,128,8,512]{3,1,2,0:T(8,128)} %copy-done.3, f32[128,4,8]{0,2,1:T(8,128)S(1)} %copy-done.11, pred[512]{0:T(512)(128)(4,1)S(1)} %copy-done.18, f32[128,4,8]{0,2,1:T(8,128)S(1)} %copy-done.16), kind=kOutput, calls=%fused_computation.26 | convolution fusion | flops 547880960 | bytes 11043328 | tf_op jit(solution)/shard_map/while/body/eval_jaxpr/rkgn,nkd->rkgd/dot_general | solution.py:71
  226.2 2.6 maximum_multiply_fusion
  229.2 0.6 copy-done.4
  229.8 2.1 fusion.69
  231.9 63.7 %all-reduce.5 = bf16[256,512]{1,0:T(8,128)(2,1)S(1)} all-reduce(f32[256,512]{1,0:T(8,128)} %fusion.69), channel_id=1, replica_groups=mesh['rep'=1,'seq'=16,'head'=2] {'seq'}, use_global_device_ids=true, to_apply=%region_8.9 | all-reduce | flops 131072 | bytes 786432 | tf_op jit(solution)/shard_map/psum | solution.py:119
  295.6 0.8 reshape.143
  296.4 0.8 copy.46
  297.5 0.4 fusion.68
  298.2 0.8 copy.70
  299.1 44.5 %reduce-scatter.6.cloned.1.call-done = f32[16,4,8,128]{3,0,2,1:T(8,128)} async-done(((f32[256,4,8,128]{3,0,2,1:T(8,128)}), f32[16,4,8,128]{3,0,2,1:T(8,128)}) %reduce-scatter.6.cloned.1.call-update) | async-done | bytes 262160 | tf_op jit(solution)/shard_map/reduce_scatter | solution.py:143
  343.5 1.4 fusion.25
  344.9 0.7 copy.86
  345.7 40.6 %all-gather.2.cloned.1.call-done = bf16[256,4096]{1,0:T(8,128)(2,1)} async-done(((bf16[16,4096]{1,0:T(8,128)(2,1)}), bf16[256,4096]{1,0:T(8,128)(2,1)}) %all-gather.2.cloned.1.call-update) | async-done | bytes 2097168 | tf_op jit(solution)/shard_map/all_gather | solution.py:155
  386.4 4.9 %fusion.70 = f32[256,512]{1,0:T(8,128)} fusion(bf16[256,4096]{1,0:T(8,128)(2,1)} %all-gather.2.cloned.1.call-done, bf16[4096,512]{1,0:T(8,128)(2,1)} %param.13), kind=kOutput, calls=%fused_computation.111 | convolution fusion | flops 1073741824 | bytes 6815744 | tf_op jit(solution)/shard_map/dot_general | solution.py:156
  391.3 13.5 %reduce-scatter.8.cloned.1.call-done = f32[256,256]{1,0:T(8,128)} async-done(((f32[256,512]{1,0:T(8,128)}), f32[256,256]{1,0:T(8,128)}) %reduce-scatter.8.cloned.1.call-update) | async-done | bytes 262160 | tf_op jit(solution)/shard_map/reduce_scatter | solution.py:157
  404.8 1.6 convert_element_type.65
  (73 shorter events, 3.0 us)
Async XLA Ops:
  6.5 1.0 copy-start
  6.5 129.2 %all-reduce.4.cloned.1.call-start = ((), (), s32[]{:S(2)}) async-start(), calls=%async_computation.7 | async-start | bytes 9437184 | tf_op jit(solution)/shard_map/psum | solution.py:119
  16.0 1.2 copy-start.6
  16.0 1.3 copy-start.20
  16.0 1.9 copy-start.7
  16.0 6.2 %copy-start.21 = (s32[2,128]{1,0:T(2,128)S(1)}, s32[2,128]{1,0:T(2,128)}, u32[]{:S(2)}) copy-start(s32[2,128]{1,0:T(2,128)} %param.16) | copy-start | bytes 3076
  16.0 282.2 %reduce-scatter.10.cloned.1.call-start = ((), (), s32[]{:S(2)}) async-start(), calls=%async_computation.6 | async-start | bytes 139264
  22.2 120.3 %copy-start.19 = (pred[512]{0:T(512)(128)(4,1)}, pred[512]{0:T(512)(128)(4,1)S(1)}, u32[]{:S(2)}) copy-start(pred[512]{0:T(512)(128)(4,1)S(1)} %get-tuple-element.92) | copy-start | bytes 1540
  143.9 3.2 copy-start.2
  143.9 4.3 %copy-start.17 = (pred[512]{0:T(512)(128)(4,1)S(1)}, pred[512]{0:T(512)(128)(4,1)}, u32[]{:S(2)}) copy-start(pred[512]{0:T(512)(128)(4,1)} %get-tuple-element.93) | copy-start | bytes 1540
  149.5 3.2 copy-start.3
  149.5 63.8 %copy-start.10 = (f32[128,4,8]{0,2,1:T(8,128)}, f32[128,4,8]{0,2,1:T(8,128)S(1)}, u32[]{:S(2)}) copy-start(f32[128,4,8]{0,2,1:T(8,128)S(1)} %broadcast_maximum_fusion.1) | copy-start | bytes 49156
  149.5 63.8 %copy-start.15 = (f32[128,4,8]{0,2,1:T(8,128)S(1)}, f32[128,4,8]{0,2,1:T(8,128)}, u32[]{:S(2)}) copy-start(f32[128,4,8]{0,2,1:T(8,128)} %get-tuple-element.78) | copy-start | bytes 49156
  149.5 65.4 %copy-start.9 = (bf16[1,512,512]{1,2,0:T(8,128)(2,1)S(1)}, bf16[1,512,512]{1,2,0:T(8,128)(2,1)}, u32[]{:S(2)}) copy-start(bf16[1,512,512]{1,2,0:T(8,128)(2,1)} %copy.74) | copy-start | bytes 1572868
  213.3 1.6 copy-start.12
  214.7 128.8 %reduce-scatter.6.cloned.1.call-start = ((), (), s32[]{:S(2)}) async-start(), calls=%async_computation.3 | async-start | bytes 4456448 | tf_op jit(solution)/shard_map/reduce_scatter | solution.py:143
  214.9 5.7 %copy-start.8 = (bf16[1,512,512]{1,2,0:T(8,128)(2,1)S(1)}, bf16[1,512,512]{1,2,0:T(8,128)(2,1)}, u32[]{:S(2)}) copy-start(bf16[1,512,512]{1,2,0:T(8,128)(2,1)} %copy.72) | copy-start | bytes 1572868
  215.0 5.7 %copy-start.11 = (f32[128,4,8]{0,2,1:T(8,128)S(1)}, f32[128,4,8]{0,2,1:T(8,128)}, u32[]{:S(2)}) copy-start(f32[128,4,8]{0,2,1:T(8,128)} %copy-done.10) | copy-start | bytes 49156
  215.0 5.7 %copy-start.16 = (f32[128,4,8]{0,2,1:T(8,128)S(1)}, f32[128,4,8]{0,2,1:T(8,128)}, u32[]{:S(2)}) copy-start(f32[128,4,8]{0,2,1:T(8,128)} %get-tuple-element.77) | copy-start | bytes 49156
  215.0 5.7 %copy-start.18 = (pred[512]{0:T(512)(128)(4,1)S(1)}, pred[512]{0:T(512)(128)(4,1)}, u32[]{:S(2)}) copy-start(pred[512]{0:T(512)(128)(4,1)} %get-tuple-element.93) | copy-start | bytes 1540
  220.7 5.5 %copy-start.14 = (f32[256,4,8]{0,2,1:T(8,128)S(1)}, f32[256,4,8]{0,2,1:T(8,128)}, u32[]{:S(2)}) copy-start(f32[256,4,8]{0,2,1:T(8,128)} %get-tuple-element.54) | copy-start | bytes 98308
  228.8 1.0 copy-start.4
  228.8 68.4 %copy-start.5 = (f32[256,4,128]{2,0,1:T(8,128)S(1)}, f32[256,4,128]{2,0,1:T(8,128)}, u32[]{:S(2)}) copy-start(f32[256,4,128]{2,0,1:T(8,128)} %get-tuple-element.39) | copy-start | bytes 1572868
  228.8 157.5 %all-gather.2.cloned.1.call-start = ((), (), s32[]{:S(2)}) async-start(), calls=%async_computation.4 | async-start | bytes 2228224 | tf_op jit(solution)/shard_map/all_gather | solution.py:155
  295.6 3.3 copy-start.13
  345.7 60.7 %copy-start.1 = (bf16[512,512]{1,0:T(8,128)(2,1)S(1)}, bf16[512,512]{1,0:T(8,128)(2,1)}, u32[]{:S(2)}) copy-start(bf16[512,512]{1,0:T(8,128)(2,1)} %param.11) | copy-start | bytes 1572868
  345.7 59.1 %reduce-scatter.8.cloned.1.call-start = ((), (), s32[]{:S(2)}) async-start(), calls=%async_computation.5 | async-start | bytes 786432 | tf_op jit(solution)/shard_map/reduce_scatter | solution.py:157
Sparse Core Ops, SparseCore 0:
  16.1 119.5 all-reduce.3
  214.8 52.9 reduce-scatter.9
  271.7 71.8 reduce-scatter.5
  345.8 40.5 all-gather.1
  391.4 13.3 reduce-scatter.7
where the time goes:
time: 414 us; the launch traced here: 413 us
  waiting for transfers between devices  209 us (50%)
  blocking collectives  124 us (30%)
  matrix products  29.4 us (7%)
  other arithmetic  20.9 us (5%)
  local copies, waits for them, and re-layouts  15.5 us (4%)
  between operations  13.6 us (3%)
    psum x1, waiting for transfers between devices, local(): q_raw, k_raw, v_raw = lax.psum((q_part, k_part, v_part), 'seq')  111 us
    psum x1, blocking collectives, local(): q_raw, k_raw, v_raw = lax.psum((q_part, k_part, v_part), 'seq')  63.7 us
    pmax x1, blocking collectives, local(): summit = lax.pmax(peak, 'seq')  60 us
    reduce_scatter x1, waiting for transfers between devices, local(): lax.psum_scatter(acc * factor[..., None], 'seq', scatter_dimension=0, til...  44.5 us
    all_gather x1, waiting for transfers between devices, local(): attention = lax.all_gather(attention_share, 'seq', axis=0, tiled=True)  40.6 us
    reduce_scatter x1, waiting for transfers between devices, local(): lax.psum_scatter(partial_value, 'head', scatter_dimension=1, tiled=True)  13.5 us
    unnamed x53, local copies, waits for them, and re-layouts  11.1 us
    dot_general x2, matrix products, step(): jnp.einsum('rkgn,nkd->rkgd', weights.astype(jnp.bfloat16), value_block, p...  11.1 us
  transfers between devices with their start and end apart: 5, of which 4 were waited for; matrix products, arithmetic and copies ran while one was open for 7% of the time, Pallas kernels for 0%

commit v1 on v0

--- a/solution.py
+++ b/solution.py
@@ -6,6 +6,14 @@
 HEAD_DIM = 128
 rope_base = 500000.0
 neg_big = -1e30
+
+
+def see_the_regions(vector, ndim_at):
+    vector = jnp.moveaxis(vector, 0, ndim_at)
+    h_now = vector.shape
+    return vector.reshape(
+        *h_now[:ndim_at], h_now[ndim_at] * h_now[ndim_at + 1], *h_now[ndim_at + 2 :]
+    )
 
 
 def ancestry(parents):
@@ -152,7 +160,14 @@
         tree_state(query_share, new_keys, new_values, allowed_share),
     )
     attention_share = (total[2] / total[1][..., None]).reshape(share, -1).astype(jnp.bfloat16)
-    attention = lax.all_gather(attention_share, "seq", axis=0, tiled=True)
+    n_lanes = lax.axis_size("seq")
+    kept_rows = [(d, (d + 1) % n_lanes) for d in range(n_lanes)]
+    pool = [attention_share]
+    while len(pool) < n_lanes:
+        pool.append(lax.ppermute(pool[-1], "seq", kept_rows))
+    x_next = lax.axis_index("seq")
+    pool = jnp.stack(pool, axis=0)[(x_next - jnp.arange(n_lanes)) % n_lanes]
+    attention = see_the_regions(pool, 0)
     partial_value = jnp.dot(attention, w_out, preferred_element_type=jnp.float32)
     return lax.psum_scatter(partial_value, "head", scatter_dimension=1, tiled=True).astype(
         jnp.bfloat16

time: 414 us -> 479 us (1.16)
  waiting for transfers between devices: 209 us -> 274 us
    ppermute x0 -> x15, waiting for transfers between devices: none -> 106 us  [local(): pool.append(lax.ppermute(pool[-1], 'seq', kept_rows))]
    all_gather x1 -> x0, waiting for transfers between devices: 40.6 us -> none  [local(): attention = lax.all_gather(attention_share, 'seq', axis=0, tiled=True)]
    unnamed x53 -> x62, local copies, waits for them, and re-layouts: 11.1 us -> 11.5 us
  transfers between devices with their start and end apart: 5 -> 19, of which waited for: 4 -> 18; matrix products, arithmetic and copies ran while one was open for 7% -> 6% of each run, Pallas kernels for 0% -> 0%
where the time goes in v1:
time: 479 us; the launch traced here: 478 us
  waiting for transfers between devices  274 us (57%)
  blocking collectives  123 us (26%)
  matrix products  28.6 us (6%)
  other arithmetic  20.4 us (4%)
  local copies, waits for them, and re-layouts  18 us (4%)
  between operations  13.7 us (3%)
    psum x1, waiting for transfers between devices, local(): q_raw, k_raw, v_raw = lax.psum((q_part, k_part, v_part), 'seq')  111 us
    ppermute x15, waiting for transfers between devices, local(): pool.append(lax.ppermute(pool[-1], 'seq', kept_rows))  106 us
    psum x1, blocking collectives, local(): q_raw, k_raw, v_raw = lax.psum((q_part, k_part, v_part), 'seq')  63.1 us
    pmax x1, blocking collectives, local(): summit = lax.pmax(peak, 'seq')  60 us
    reduce_scatter x1, waiting for transfers between devices, local(): lax.psum_scatter(acc * factor[..., None], 'seq', scatter_dimension=0, til...  45.1 us
    reduce_scatter x1, waiting for transfers between devices, local(): lax.psum_scatter(partial_value, 'head', scatter_dimension=1, tiled=True)  12 us
    unnamed x62, local copies, waits for them, and re-layouts  11.5 us
    dot_general x2, matrix products, step(): jnp.einsum('rkgn,nkd->rkgd', weights.astype(jnp.bfloat16), value_block, p...  11.2 us
  transfers between devices with their start and end apart: 19, of which 18 were waited for; matrix products, arithmetic and copies ran while one was open for 6% of the time, Pallas kernels for 0%

profile of v1, /device:TPU:0, one launch (start us, length us, event | category | flops | bytes accessed | tf_op | source)
XLA Modules:
  0.0 478.2 jit_solution(2876978829322091860)
XLA Ops:
  6.5 1.0 copy-done
  7.6 1.2 convolution_bitcast_fusion.1
  8.8 0.9 copy.86
  9.7 3.5 convolution_bitcast_fusion
  13.3 2.7 copy.78
  16.1 1.1 copy-done.7
  18.1 1.0 copy.76
  19.3 1.0 copy.74
  20.5 1.8 fusion.47
  25.1 110.7 %all-reduce.4.cloned.1.call-done = (f32[256,4,128]{2,0,1:T(8,128)}, f32[256,32,128]{2,1,0:T(8,128)}) async-done(((f32[256,4,128]{2,0,1:T(8,128)}, f32[256,32,128]{2,1,0:T(8,128)}), (f32[256,4,128]{2,0,1:T(8,128)}, f32[256,32,128]{2,1,0:T(8,128)})) %all-reduce.4.cloned.1.call-update) | async-done | bytes 4718608 | tf_op jit(solution)/shard_map/psum | solution.py:127
  135.8 4.9 %multiply_subtract_fusion = (bf16[256,32,64]{2,1,0:T(8,128)(2,1)S(1)}, bf16[256,32,64]{2,1,0:T(8,128)(2,1)S(1)}) fusion(f32[256,32,128]{2,1,0:T(8,128)} %get-tuple-element.40, f32[256,64]{1,0:T(8,128)S(1)} %get-tuple-element.81, f32[256,64]{1,0:T(8,128)S(1)} %get-tuple-element.80), kind=kLoop, calls=%fused_computation.18 | loop fusion | flops 4194304 | bytes 6422528 | tf_op jit(solution)/shard_map/sub | solution.py:43
  140.7 1.2 maximum_convert_fusion
  142.7 1.3 bitcast_reduce_fusion
  144.0 2.4 fusion.6
  146.4 0.8 copy-done.2
  148.3 1.3 bitcast_reduce_fusion.1
  149.6 2.4 fusion.4
  152.0 0.8 copy-done.3
  153.4 60.0 %pmax.7 = f32[256,4,8]{0,2,1:T(8,128)S(1)} all-reduce(f32[256,4,8]{0,2,1:T(8,128)S(1)} %pad_maximum_fusion), channel_id=1, replica_groups=mesh['rep'=1,'seq'=16,'head'=2] {'seq'}, use_global_device_ids=true, to_apply=%region_4.5 | all-reduce | flops 8192 | bytes 65536 | tf_op jit(solution)/shard_map/pmax | solution.py:147
  214.5 5.7 %bitcast_add_fusion = f32[128,4,8,128]{3,0,2,1:T(8,128)S(1)} fusion(bf16[512,4,128,1]{0,2,3,1:T(8,128)(2,1)S(1)} %bitcast.177, f32[4,128,8,512]{3,1,2,0:T(8,128)} %copy-done.2, f32[128,4,8]{0,2,1:T(8,128)S(1)} %broadcast_maximum_fusion, pred[512]{0:T(512)(128)(4,1)} %copy-done.16, f32[128,4,8]{0,2,1:T(8,128)} %get-tuple-element.79), kind=kOutput, calls=%fused_computation.26 | convolution fusion | flops 547880960 | bytes 11043328 | tf_op jit(solution)/shard_map/while/body/eval_jaxpr/rkgn,nkd->rkgd/dot_general | solution.py:79
  220.3 5.5 %bitcast_add_fusion.1 = f32[128,4,8,128]{3,0,2,1:T(8,128)S(1)} fusion(bf16[512,4,128,1]{0,2,3,1:T(8,128)(2,1)S(1)} %bitcast.176, f32[4,128,8,512]{3,1,2,0:T(8,128)} %copy-done.3, f32[128,4,8]{0,2,1:T(8,128)S(1)} %broadcast_maximum_fusion.1, pred[512]{0:T(512)(128)(4,1)S(1)} %copy-done.15, f32[128,4,8]{0,2,1:T(8,128)S(1)} %copy-done.13), kind=kOutput, calls=%fused_computation.27 | convolution fusion | flops 547880960 | bytes 11043328 | tf_op jit(solution)/shard_map/while/body/eval_jaxpr/rkgn,nkd->rkgd/dot_general | solution.py:79
  225.7 2.6 maximum_multiply_fusion
  229.3 1.3 fusion.71
  230.7 63.1 %all-reduce.5 = bf16[256,512]{1,0:T(8,128)(2,1)S(1)} all-reduce(f32[256,512]{1,0:T(8,128)S(1)} %fusion.71), channel_id=1, replica_groups=mesh['rep'=1,'seq'=16,'head'=2] {'seq'}, use_global_device_ids=true, to_apply=%region_8.9 | all-reduce | flops 131072 | bytes 786432 | tf_op jit(solution)/shard_map/psum | solution.py:127
  294.6 0.8 copy.47
  295.4 1.1 subtract_convert_fusion
  297.2 0.8 copy.72
  298.1 45.1 %reduce-scatter.6.cloned.1.call-done = f32[16,4,8,128]{3,0,2,1:T(8,128)} async-done(((f32[256,4,8,128]{3,0,2,1:T(8,128)}), f32[16,4,8,128]{3,0,2,1:T(8,128)}) %reduce-scatter.6.cloned.1.call-update) | async-done | bytes 262160 | tf_op jit(solution)/shard_map/reduce_scatter | solution.py:151
  343.2 1.3 fusion.25
  344.8 7.1 %collective-permute-done = bf16[16,4096]{1,0:T(8,128)(2,1)S(1)} collective-permute-done((bf16[16,4096]{1,0:T(8,128)(2,1)S(1)}, bf16[16,4096]{1,0:T(8,128)(2,1)S(1)}, u32[]{:S(2)}, u32[]{:S(2)}) %collective-permute-start) | collective-permute-done | bytes 131104 | tf_op jit(solution)/shard_map/ppermute | solution.py:167
  351.8 7.1 %collective-permute-done.1 = bf16[16,4096]{1,0:T(8,128)(2,1)S(1)} collective-permute-done((bf16[16,4096]{1,0:T(8,128)(2,1)S(1)}, bf16[16,4096]{1,0:T(8,128)(2,1)S(1)}, u32[]{:S(2)}, u32[]{:S(2)}) %collective-permute-start.1) | collective-permute-done | bytes 131104 | tf_op jit(solution)/shard_map/ppermute | solution.py:167
  358.9 7.1 %collective-permute-done.2 = bf16[16,4096]{1,0:T(8,128)(2,1)S(1)} collective-permute-done((bf16[16,4096]{1,0:T(8,128)(2,1)S(1)}, bf16[16,4096]{1,0:T(8,128)(2,1)S(1)}, u32[]{:S(2)}, u32[]{:S(2)}) %collective-permute-start.2) | collective-permute-done | bytes 131104 | tf_op jit(solution)/shard_map/ppermute | solution.py:167
  366.0 7.1 %collective-permute-done.3 = bf16[16,4096]{1,0:T(8,128)(2,1)S(1)} collective-permute-done((bf16[16,4096]{1,0:T(8,128)(2,1)S(1)}, bf16[16,4096]{1,0:T(8,128)(2,1)S(1)}, u32[]{:S(2)}, u32[]{:S(2)}) %collective-permute-start.3) | collective-permute-done | bytes 131104 | tf_op jit(solution)/shard_map/ppermute | solution.py:167
  373.1 7.1 %collective-permute-done.4 = bf16[16,4096]{1,0:T(8,128)(2,1)S(1)} collective-permute-done((bf16[16,4096]{1,0:T(8,128)(2,1)S(1)}, bf16[16,4096]{1,0:T(8,128)(2,1)S(1)}, u32[]{:S(2)}, u32[]{:S(2)}) %collective-permute-start.4) | collective-permute-done | bytes 131104 | tf_op jit(solution)/shard_map/ppermute | solution.py:167
  380.2 7.1 %collective-permute-done.5 = bf16[16,4096]{1,0:T(8,128)(2,1)S(1)} collective-permute-done((bf16[16,4096]{1,0:T(8,128)(2,1)S(1)}, bf16[16,4096]{1,0:T(8,128)(2,1)S(1)}, u32[]{:S(2)}, u32[]{:S(2)}) %collective-permute-start.5) | collective-permute-done | bytes 131104 | tf_op jit(solution)/shard_map/ppermute | solution.py:167
  387.3 7.1 %collective-permute-done.6 = bf16[16,4096]{1,0:T(8,128)(2,1)S(1)} collective-permute-done((bf16[16,4096]{1,0:T(8,128)(2,1)S(1)}, bf16[16,4096]{1,0:T(8,128)(2,1)S(1)}, u32[]{:S(2)}, u32[]{:S(2)}) %collective-permute-start.6) | collective-permute-done | bytes 131104 | tf_op jit(solution)/shard_map/ppermute | solution.py:167
  394.4 7.1 %collective-permute-done.7 = bf16[16,4096]{1,0:T(8,128)(2,1)S(1)} collective-permute-done((bf16[16,4096]{1,0:T(8,128)(2,1)S(1)}, bf16[16,4096]{1,0:T(8,128)(2,1)S(1)}, u32[]{:S(2)}, u32[]{:S(2)}) %collective-permute-start.7) | collective-permute-done | bytes 131104 | tf_op jit(solution)/shard_map/ppermute | solution.py:167
  401.5 7.1 %collective-permute-done.8 = bf16[16,4096]{1,0:T(8,128)(2,1)S(1)} collective-permute-done((bf16[16,4096]{1,0:T(8,128)(2,1)S(1)}, bf16[16,4096]{1,0:T(8,128)(2,1)S(1)}, u32[]{:S(2)}, u32[]{:S(2)}) %collective-permute-start.8) | collective-permute-done | bytes 131104 | tf_op jit(solution)/shard_map/ppermute | solution.py:167
  408.6 7.1 %collective-permute-done.9 = bf16[16,4096]{1,0:T(8,128)(2,1)S(1)} collective-permute-done((bf16[16,4096]{1,0:T(8,128)(2,1)S(1)}, bf16[16,4096]{1,0:T(8,128)(2,1)S(1)}, u32[]{:S(2)}, u32[]{:S(2)}) %collective-permute-start.9) | collective-permute-done | bytes 131104 | tf_op jit(solution)/shard_map/ppermute | solution.py:167
  415.6 7.1 %collective-permute-done.10 = bf16[16,4096]{1,0:T(8,128)(2,1)S(1)} collective-permute-done((bf16[16,4096]{1,0:T(8,128)(2,1)S(1)}, bf16[16,4096]{1,0:T(8,128)(2,1)S(1)}, u32[]{:S(2)}, u32[]{:S(2)}) %collective-permute-start.10) | collective-permute-done | bytes 131104 | tf_op jit(solution)/shard_map/ppermute | solution.py:167
  422.7 7.1 %collective-permute-done.11 = bf16[16,4096]{1,0:T(8,128)(2,1)S(1)} collective-permute-done((bf16[16,4096]{1,0:T(8,128)(2,1)S(1)}, bf16[16,4096]{1,0:T(8,128)(2,1)S(1)}, u32[]{:S(2)}, u32[]{:S(2)}) %collective-permute-start.11) | collective-permute-done | bytes 131104 | tf_op jit(solution)/shard_map/ppermute | solution.py:167
  429.8 7.1 %collective-permute-done.12 = bf16[16,4096]{1,0:T(8,128)(2,1)S(1)} collective-permute-done((bf16[16,4096]{1,0:T(8,128)(2,1)S(1)}, bf16[16,4096]{1,0:T(8,128)(2,1)S(1)}, u32[]{:S(2)}, u32[]{:S(2)}) %collective-permute-start.12) | collective-permute-done | bytes 131104 | tf_op jit(solution)/shard_map/ppermute | solution.py:167
  436.9 7.1 %collective-permute-done.13 = bf16[16,4096]{1,0:T(8,128)(2,1)S(1)} collective-permute-done((bf16[16,4096]{1,0:T(8,128)(2,1)S(1)}, bf16[16,4096]{1,0:T(8,128)(2,1)S(1)}, u32[]{:S(2)}, u32[]{:S(2)}) %collective-permute-start.13) | collective-permute-done | bytes 131104 | tf_op jit(solution)/shard_map/ppermute | solution.py:167
  444.0 7.1 %collective-permute-done.14 = bf16[16,4096]{1,0:T(8,128)(2,1)S(1)} collective-permute-done((bf16[16,4096]{1,0:T(8,128)(2,1)S(1)}, bf16[16,4096]{1,0:T(8,128)(2,1)S(1)}, u32[]{:S(2)}, u32[]{:S(2)}) %collective-permute-start.14) | collective-permute-done | bytes 131104 | tf_op jit(solution)/shard_map/ppermute | solution.py:167
  451.1 2.0 gather_fusion
  453.1 4.9 %fusion.72 = f32[256,512]{1,0:T(8,128)} fusion(bf16[256,4096]{1,0:T(8,128)(2,1)} %bitcast.174, bf16[4096,512]{1,0:T(8,128)(2,1)} %param.13), kind=kOutput, calls=%fused_computation.135 | convolution fusion | flops 1073741824 | bytes 6815744 | tf_op jit(solution)/shard_map/dot_general | solution.py:171
  458.0 12.0 %reduce-scatter.8.cloned.1.call-done = f32[256,256]{1,0:T(8,128)} async-done(((f32[256,512]{1,0:T(8,128)}), f32[256,256]{1,0:T(8,128)}) %reduce-scatter.8.cloned.1.call-update) | async-done | bytes 262160 | tf_op jit(solution)/shard_map/reduce_scatter | solution.py:172
  470.1 1.6 convert_element_type.76
  (114 shorter events, 10.4 us)
Async XLA Ops:
  6.5 1.0 copy-start
  6.5 129.3 %all-reduce.4.cloned.1.call-start = ((), (), s32[]{:S(2)}) async-start(), calls=%async_computation.6 | async-start | bytes 9437184 | tf_op jit(solution)/shard_map/psum | solution.py:127
  16.0 1.2 copy-start.7
  16.0 1.3 copy-start.17
  16.0 2.0 copy-start.8
  16.0 6.3 %copy-start.18 = (s32[2,128]{1,0:T(2,128)S(1)}, s32[2,128]{1,0:T(2,128)}, u32[]{:S(2)}) copy-start(s32[2,128]{1,0:T(2,128)} %param.16) | copy-start | bytes 3076
  16.1 281.2 %reduce-scatter.10.cloned.1.call-start = ((), (), s32[]{:S(2)}) async-start(), calls=%async_computation.5 | async-start | bytes 139264
  22.3 121.7 %copy-start.16 = (pred[512]{0:T(512)(128)(4,1)}, pred[512]{0:T(512)(128)(4,1)S(1)}, u32[]{:S(2)}) copy-start(pred[512]{0:T(512)(128)(4,1)S(1)} %get-tuple-element.92) | copy-start | bytes 1540
  25.1 115.7 %copy-start.6 = (f32[256,64]{1,0:T(8,128)}, f32[256,64]{1,0:T(8,128)S(1)}, u32[]{:S(2)}) copy-start(f32[256,64]{1,0:T(8,128)S(1)} %get-tuple-element.81) | copy-start | bytes 196612
  144.0 3.2 copy-start.2
  144.0 4.2 copy-start.14
  149.6 3.3 copy-start.3
  149.6 64.8 %copy-start.10 = (bf16[1,512,512]{1,2,0:T(8,128)(2,1)S(1)}, bf16[1,512,512]{1,2,0:T(8,128)(2,1)}, u32[]{:S(2)}) copy-start(bf16[1,512,512]{1,2,0:T(8,128)(2,1)} %copy.76) | copy-start | bytes 1572868
  213.4 6.8 %copy-start.11 = (f32[256,4,8]{0,2,1:T(8,128)}, f32[256,4,8]{0,2,1:T(8,128)S(1)}, u32[]{:S(2)}) copy-start(f32[256,4,8]{0,2,1:T(8,128)S(1)} %pmax.7) | copy-start | bytes 98308
  214.2 129.0 %reduce-scatter.6.cloned.1.call-start = ((), (), s32[]{:S(2)}) async-start(), calls=%async_computation.3 | async-start | bytes 4456448 | tf_op jit(solution)/shard_map/reduce_scatter | solution.py:151
  214.4 5.8 %copy-start.9 = (bf16[1,512,512]{1,2,0:T(8,128)(2,1)S(1)}, bf16[1,512,512]{1,2,0:T(8,128)(2,1)}, u32[]{:S(2)}) copy-start(bf16[1,512,512]{1,2,0:T(8,128)(2,1)} %copy.74) | copy-start | bytes 1572868
  214.5 5.8 %copy-start.13 = (f32[128,4,8]{0,2,1:T(8,128)S(1)}, f32[128,4,8]{0,2,1:T(8,128)}, u32[]{:S(2)}) copy-start(f32[128,4,8]{0,2,1:T(8,128)} %get-tuple-element.77) | copy-start | bytes 49156
  214.5 5.8 %copy-start.15 = (pred[512]{0:T(512)(128)(4,1)S(1)}, pred[512]{0:T(512)(128)(4,1)}, u32[]{:S(2)}) copy-start(pred[512]{0:T(512)(128)(4,1)} %get-tuple-element.93) | copy-start | bytes 1540
  228.3 1.0 copy-start.4
  228.3 67.1 %copy-start.5 = (f32[256,4,128]{2,0,1:T(8,128)S(1)}, f32[256,4,128]{2,0,1:T(8,128)}, u32[]{:S(2)}) copy-start(f32[256,4,128]{2,0,1:T(8,128)} %get-tuple-element.39) | copy-start | bytes 1572868
  228.3 241.7 %reduce-scatter.8.cloned.1.call-start = ((), (), s32[]{:S(2)}) async-start(), calls=%async_computation.4 | async-start | bytes 786432 | tf_op jit(solution)/shard_map/reduce_scatter | solution.py:172
  293.8 4.2 copy-start.12
  344.7 7.1 %collective-permute-start = (bf16[16,4096]{1,0:T(8,128)(2,1)S(1)}, bf16[16,4096]{1,0:T(8,128)(2,1)S(1)}, u32[]{:S(2)}, u32[]{:S(2)}) collective-permute-start(bf16[16,4096]{1,0:T(8,128)(2,1)S(1)} %bitcast.180), channel_id=1, source_target_pairs={{0,2},{2,4},{4,6},{6,8},{8,10},{10,12},{12,14},{14,16},{16,18},{18... | collective-permute-start | bytes 393224 | tf_op jit(solution)/shard_map/ppermute | solution.py:167
  351.8 7.1 %collective-permute-start.1 = (bf16[16,4096]{1,0:T(8,128)(2,1)S(1)}, bf16[16,4096]{1,0:T(8,128)(2,1)S(1)}, u32[]{:S(2)}, u32[]{:S(2)}) collective-permute-start(bf16[16,4096]{1,0:T(8,128)(2,1)S(1)} %collective-permute-done), channel_id=1, source_target_pairs={{0,2},{2,4},{4,6},{6,8},{8,10},{10,12},{12,14},{14,16},{16,18},{18... | collective-permute-start | bytes 393224 | tf_op jit(solution)/shard_map/ppermute | solution.py:167
  358.9 7.1 %collective-permute-start.2 = (bf16[16,4096]{1,0:T(8,128)(2,1)S(1)}, bf16[16,4096]{1,0:T(8,128)(2,1)S(1)}, u32[]{:S(2)}, u32[]{:S(2)}) collective-permute-start(bf16[16,4096]{1,0:T(8,128)(2,1)S(1)} %collective-permute-done.1), channel_id=1, source_target_pairs={{0,2},{2,4},{4,6},{6,8},{8,10},{10,12},{12,14},{14,16},{16,18},{18... | collective-permute-start | bytes 393224 | tf_op jit(solution)/shard_map/ppermute | solution.py:167
  366.0 7.1 %collective-permute-start.3 = (bf16[16,4096]{1,0:T(8,128)(2,1)S(1)}, bf16[16,4096]{1,0:T(8,128)(2,1)S(1)}, u32[]{:S(2)}, u32[]{:S(2)}) collective-permute-start(bf16[16,4096]{1,0:T(8,128)(2,1)S(1)} %collective-permute-done.2), channel_id=1, source_target_pairs={{0,2},{2,4},{4,6},{6,8},{8,10},{10,12},{12,14},{14,16},{16,18},{18... | collective-permute-start | bytes 393224 | tf_op jit(solution)/shard_map/ppermute | solution.py:167
  373.1 7.1 %collective-permute-start.4 = (bf16[16,4096]{1,0:T(8,128)(2,1)S(1)}, bf16[16,4096]{1,0:T(8,128)(2,1)S(1)}, u32[]{:S(2)}, u32[]{:S(2)}) collective-permute-start(bf16[16,4096]{1,0:T(8,128)(2,1)S(1)} %collective-permute-done.3), channel_id=1, source_target_pairs={{0,2},{2,4},{4,6},{6,8},{8,10},{10,12},{12,14},{14,16},{16,18},{18... | collective-permute-start | bytes 393224 | tf_op jit(solution)/shard_map/ppermute | solution.py:167
  380.2 7.1 %collective-permute-start.5 = (bf16[16,4096]{1,0:T(8,128)(2,1)S(1)}, bf16[16,4096]{1,0:T(8,128)(2,1)S(1)}, u32[]{:S(2)}, u32[]{:S(2)}) collective-permute-start(bf16[16,4096]{1,0:T(8,128)(2,1)S(1)} %collective-permute-done.4), channel_id=1, source_target_pairs={{0,2},{2,4},{4,6},{6,8},{8,10},{10,12},{12,14},{14,16},{16,18},{18... | collective-permute-start | bytes 393224 | tf_op jit(solution)/shard_map/ppermute | solution.py:167
  387.3 7.1 %collective-permute-start.6 = (bf16[16,4096]{1,0:T(8,128)(2,1)S(1)}, bf16[16,4096]{1,0:T(8,128)(2,1)S(1)}, u32[]{:S(2)}, u32[]{:S(2)}) collective-permute-start(bf16[16,4096]{1,0:T(8,128)(2,1)S(1)} %collective-permute-done.5), channel_id=1, source_target_pairs={{0,2},{2,4},{4,6},{6,8},{8,10},{10,12},{12,14},{14,16},{16,18},{18... | collective-permute-start | bytes 393224 | tf_op jit(solution)/shard_map/ppermute | solution.py:167
  394.4 7.1 %collective-permute-start.7 = (bf16[16,4096]{1,0:T(8,128)(2,1)S(1)}, bf16[16,4096]{1,0:T(8,128)(2,1)S(1)}, u32[]{:S(2)}, u32[]{:S(2)}) collective-permute-start(bf16[16,4096]{1,0:T(8,128)(2,1)S(1)} %collective-permute-done.6), channel_id=1, source_target_pairs={{0,2},{2,4},{4,6},{6,8},{8,10},{10,12},{12,14},{14,16},{16,18},{18... | collective-permute-start | bytes 393224 | tf_op jit(solution)/shard_map/ppermute | solution.py:167
  401.4 7.1 %collective-permute-start.8 = (bf16[16,4096]{1,0:T(8,128)(2,1)S(1)}, bf16[16,4096]{1,0:T(8,128)(2,1)S(1)}, u32[]{:S(2)}, u32[]{:S(2)}) collective-permute-start(bf16[16,4096]{1,0:T(8,128)(2,1)S(1)} %collective-permute-done.7), channel_id=1, source_target_pairs={{0,2},{2,4},{4,6},{6,8},{8,10},{10,12},{12,14},{14,16},{16,18},{18... | collective-permute-start | bytes 393224 | tf_op jit(solution)/shard_map/ppermute | solution.py:167
  408.5 7.1 %collective-permute-start.9 = (bf16[16,4096]{1,0:T(8,128)(2,1)S(1)}, bf16[16,4096]{1,0:T(8,128)(2,1)S(1)}, u32[]{:S(2)}, u32[]{:S(2)}) collective-permute-start(bf16[16,4096]{1,0:T(8,128)(2,1)S(1)} %collective-permute-done.8), channel_id=1, source_target_pairs={{0,2},{2,4},{4,6},{6,8},{8,10},{10,12},{12,14},{14,16},{16,18},{18... | collective-permute-start | bytes 393224 | tf_op jit(solution)/shard_map/ppermute | solution.py:167
  415.6 7.1 %collective-permute-start.10 = (bf16[16,4096]{1,0:T(8,128)(2,1)S(1)}, bf16[16,4096]{1,0:T(8,128)(2,1)S(1)}, u32[]{:S(2)}, u32[]{:S(2)}) collective-permute-start(bf16[16,4096]{1,0:T(8,128)(2,1)S(1)} %collective-permute-done.9), channel_id=1, source_target_pairs={{0,2},{2,4},{4,6},{6,8},{8,10},{10,12},{12,14},{14,16},{16,18},{18... | collective-permute-start | bytes 393224 | tf_op jit(solution)/shard_map/ppermute | solution.py:167
  422.7 7.1 %collective-permute-start.11 = (bf16[16,4096]{1,0:T(8,128)(2,1)S(1)}, bf16[16,4096]{1,0:T(8,128)(2,1)S(1)}, u32[]{:S(2)}, u32[]{:S(2)}) collective-permute-start(bf16[16,4096]{1,0:T(8,128)(2,1)S(1)} %collective-permute-done.10), channel_id=1, source_target_pairs={{0,2},{2,4},{4,6},{6,8},{8,10},{10,12},{12,14},{14,16},{16,18},{18... | collective-permute-start | bytes 393224 | tf_op jit(solution)/shard_map/ppermute | solution.py:167
  429.8 7.1 %collective-permute-start.12 = (bf16[16,4096]{1,0:T(8,128)(2,1)S(1)}, bf16[16,4096]{1,0:T(8,128)(2,1)S(1)}, u32[]{:S(2)}, u32[]{:S(2)}) collective-permute-start(bf16[16,4096]{1,0:T(8,128)(2,1)S(1)} %collective-permute-done.11), channel_id=1, source_target_pairs={{0,2},{2,4},{4,6},{6,8},{8,10},{10,12},{12,14},{14,16},{16,18},{18... | collective-permute-start | bytes 393224 | tf_op jit(solution)/shard_map/ppermute | solution.py:167
  436.9 7.1 %collective-permute-start.13 = (bf16[16,4096]{1,0:T(8,128)(2,1)S(1)}, bf16[16,4096]{1,0:T(8,128)(2,1)S(1)}, u32[]{:S(2)}, u32[]{:S(2)}) collective-permute-start(bf16[16,4096]{1,0:T(8,128)(2,1)S(1)} %collective-permute-done.12), channel_id=1, source_target_pairs={{0,2},{2,4},{4,6},{6,8},{8,10},{10,12},{12,14},{14,16},{16,18},{18... | collective-permute-start | bytes 393224 | tf_op jit(solution)/shard_map/ppermute | solution.py:167
  444.0 7.1 %collective-permute-start.14 = (bf16[16,4096]{1,0:T(8,128)(2,1)S(1)}, bf16[16,4096]{1,0:T(8,128)(2,1)S(1)}, u32[]{:S(2)}, u32[]{:S(2)}) collective-permute-start(bf16[16,4096]{1,0:T(8,128)(2,1)S(1)} %collective-permute-done.13), channel_id=1, source_target_pairs={{0,2},{2,4},{4,6},{6,8},{8,10},{10,12},{12,14},{14,16},{16,18},{18... | collective-permute-start | bytes 393224 | tf_op jit(solution)/shard_map/ppermute | solution.py:167
  453.1 18.6 %copy-start.1 = (bf16[512,512]{1,0:T(8,128)(2,1)S(1)}, bf16[512,512]{1,0:T(8,128)(2,1)}, u32[]{:S(2)}) copy-start(bf16[512,512]{1,0:T(8,128)(2,1)} %param.11) | copy-start | bytes 1572868
Sparse Core Ops, SparseCore 0:
  16.2 119.5 all-reduce.3
  214.3 52.8 reduce-scatter.9
  271.1 72.0 reduce-scatter.5
  458.2 11.8 reduce-scatter.7
